TPU v7x, 32 devices: a whole 2x2x4 slice. The times are simulated.
32 devices in a mesh: cx: 2 (over x), cyz: 4 (over z), vert: 4 (over y, core).
Axes of the slice: x: 2, y: 2, z: 4, core: 2. Of those that a mesh axis runs over, the one named last changes fastest.
Arguments:
- dist: float32 [1728, 8, 32, 128], P('vert', 'cx', 'cyz'), may hold values from -40 to 40
- cell_type: int32 [8, 32, 128], P('cx', 'cyz'), may hold values from 0 to 3, as said below
- basis: float32 [13, 1728], P(None, 'vert'), may hold values from -0.15625 to 0.15625
- backmap: float32 [1728, 13], P('vert'), may hold values from -1.75 to 1.75
- source_map: float32 [13, 13], replicated, may hold values from -1.75 to 1.75
- coupling: float32 [13, 13], replicated, may hold values from -0.06 to 0.06
- diffusivity: float32 [13], replicated, may hold values from 0.5 to 8
- gradient_gain: float32 [13], replicated, may hold values from 0.1 to 1
Outputs:
- new_dist: bfloat16 [1728, 8, 32, 128], P('vert', 'cx', 'cyz')
- norms: float32 [5, 13], replicated
Inputs may be any that keep to these rules, and one draw needn't show every extreme that they name: `cell_type`: 0 fluid, 1 wall, 2 inlet, 3 outlet; most cells are fluid.
All inputs are finite; a program needn't handle non-finite values.
Results may differ from a plain program's by a relative error of at most 0.001.
Values sent between devices are 32-bit elements; how exact they have to be, the bound alone decides.
A program may use at most 64 MiB of HBM per device.

v0:
```python
import math

import jax
import jax.numpy as jnp
from jax import lax
from jax.sharding import PartitionSpec as P

ITERS = 4


highest = lax.Precision.HIGHEST


def with_halo(x, sides, width):
    for axis, dim in sides:
        size, length = (lax.axis_size(axis), x.shape[dim])
        up = [(i, (i + 1) % size) for i in range(size - 1)]
        down = [(j, i) for i, j in up]
        last = lax.slice_in_dim(x, length - width, length, axis=dim)
        leading = lax.slice_in_dim(x, 0, width, axis=dim)
        before = lax.ppermute(last, axis, up)
        after = lax.ppermute(leading, axis, down)
        x = jnp.concatenate([before, x, after], axis=dim)
    return x


def laplace(field):
    padded = with_halo(field, (("cx", 1), ("cyz", 2)), 1)
    z_padded = jnp.pad(field, ((0, 0), (0, 0), (0, 0), (1, 1)))
    near = padded[:, 2:, 1:-1, :] + padded[:, :-2, 1:-1, :]
    near = near + padded[:, 1:-1, 2:, :] + padded[:, 1:-1, :-2, :]
    near = near + z_padded[:, :, :, 2:] + z_padded[:, :, :, :-2]
    return 6.0 * field - near


def own_squares(resid):
    rows = resid.shape[2] // lax.axis_size("vert")
    share = lax.dynamic_slice_in_dim(resid, lax.axis_index("vert") * rows, rows, 2)
    return jnp.sum(share * share, axis=(1, 2, 3))


def summed_squares(local_sums):
    return lax.psum(local_sums, ("cx", "cyz", "vert"))


def local(dist, cell_type, basis, backmap, source_map, coupling, diffusivity, gradient_gain):
    vel_local = dist.shape[0]
    block_x, block_y, block_z = (dist.shape[1], dist.shape[2], dist.shape[3])
    field_count = basis.shape[0]
    partial_value = jnp.dot(basis, dist.reshape(vel_local, -1), precision=highest)
    partial_value = partial_value.reshape(field_count, block_x, block_y, block_z)
    moments = lax.psum(partial_value, "vert")
    fluid = (cell_type == 0).astype(jnp.float32)[None]
    inlet = (cell_type == 2).astype(jnp.float32)[None]
    outlet = (cell_type == 3).astype(jnp.float32)[None]
    active = fluid + outlet
    diffuse = diffusivity[:, None, None, None]
    mixed_source = jnp.einsum("cj,jxyz->cxyz", source_map, moments, precision=highest)
    target = (
        active * (mixed_source - gradient_gain[:, None, None, None] * laplace(moments))
        + inlet * moments
    )
    diagonal = 1.0 + 6.0 * active * diffuse - fluid * jnp.diag(coupling)[:, None, None, None]
    correction = jnp.zeros_like(target)
    resid = target
    squares = []
    for sweep in range(ITERS):
        squares.append(summed_squares(own_squares(resid)))
        omega = 1.0 / (1.0 + 0.8 * math.cos(math.pi * (2 * sweep + 1) / (2 * ITERS)))
        correction = correction + omega * resid / diagonal
        coupled = jnp.einsum("cj,jxyz->cxyz", coupling, correction, precision=highest)
        resid = target - (correction + active * diffuse * laplace(correction) - fluid * coupled)
    squares.append(summed_squares(own_squares(resid)))
    totals = jnp.stack(squares)
    cell_total = block_x * block_y * block_z * lax.axis_size("cx") * lax.axis_size("cyz")
    norms = jnp.sqrt(totals / cell_total + 1e-06)
    delta = jnp.dot(backmap, correction.reshape(field_count, -1), precision=highest)
    new_dist = (dist + delta.reshape(dist.shape)).astype(jnp.bfloat16)
    return (new_dist, norms)


def solution(mesh):
    placed = (
        P("vert", "cx", "cyz", None),
        P("cx", "cyz", None),
        P(None, "vert"),
        P("vert", None),
        P(),
        P(),
        P(),
        P(),
    )
    return jax.shard_map(
        local,
        mesh=mesh,
        in_specs=placed,
        out_specs=(P("vert", "cx", "cyz", None), P()),
        check_vma=False,
    )
```

profile of v0, /device:TPU:0, one launch (start us, length us, event | category | flops | bytes accessed | tf_op | source)
XLA Modules:
  0.0 210.2 jit_solution(10340321448121966923)
XLA Ops:
  7.2 0.0 copy-start
  7.2 0.0 all-reduce.8.cloned.1.call-start
  7.2 9.8 %copy.23 = f32[54,8,32,128]{3,1,2,0:T(8,128)S(1)} copy(f32[54,8,32,128]{3,2,1,0:T(8,128)} %bitcast.95) | data formatting | bytes 14155776
  17.0 1.5 copy.16
  18.6 8.2 %fusion = f32[13,4,8,128]{3,0,2,1:T(8,128)} fusion(f32[4,8,128,432]{2,1,0,3:T(8,128)S(1)} %bitcast.98, f32[13,432]{1,0:T(8,128)S(1)} %copy-done.3), kind=kOutput, calls=%fused_computation.2 | convolution fusion | flops 276037632 | bytes 7313344 | tf_op jit(solution)/shard_map/dot_general | solution.py:50
  26.7 0.0 all-reduce.8.cloned.1.call-update
  26.8 35.1 %all-reduce.8.cloned.1.call-done = f32[13,4,8,128]{3,0,2,1:T(8,128)} async-done(((f32[13,4,8,128]{3,0,2,1:T(8,128)}), f32[13,4,8,128]{3,0,2,1:T(8,128)}) %all-reduce.8.cloned.1.call-update) | async-done | bytes 213008 | tf_op jit(solution)/shard_map/psum | solution.py:52
  61.9 0.9 fusion.64
  62.8 3.4 %collective-permute-start.1 = (f32[13,1,8,128]{3,0,2,1:T(8,128)S(1)}, f32[13,1,8,128]{3,0,2,1:T(8,128)S(1)}, u32[]{:S(2)}, u32[]{:S(2)}) collective-permute-start(f32[13,1,8,128]{3,0,2,1:T(8,128)S(1)} %get-tuple-element.30), channel_id=1, source_target_pairs={{0,16},{1,17},{2,18},{3,19},{4,20},{5,21},{6,22},{7,23},{8,24},{9,... | collective-permute-start | bytes 159752 | tf_op jit(solution)/shard_map/ppermute | solution.py:21
  66.2 1.3 collective-permute-start
  67.5 0.6 collective-permute-done.1
  68.1 1.0 constant_dynamic-update-slice_fusion.1
  69.1 3.3 %collective-permute-done = f32[13,1,8,128]{3,0,2,1:T(8,128)S(1)} collective-permute-done((f32[13,1,8,128]{3,0,2,1:T(8,128)S(1)}, f32[13,1,8,128]{3,0,2,1:T(8,128)S(1)}, u32[]{:S(2)}, u32[]{:S(2)}) %collective-permute-start) | collective-permute-done | bytes 53280 | tf_op jit(solution)/shard_map/ppermute | solution.py:22
  72.4 1.3 collective-permute-start.2
  73.7 4.5 %collective-permute-start.3 = (f32[13,6,1,128]{3,0,2,1:T(8,128)S(1)}, f32[13,6,1,128]{3,0,2,1:T(8,128)S(1)}, u32[]{:S(2)}, u32[]{:S(2)}) collective-permute-start(f32[13,6,1,128]{3,0,2,1:T(8,128)S(1)} %get-tuple-element.18), channel_id=1, source_target_pairs={{0,4},{4,8},{8,12},{1,5},{5,9},{9,13},{2,6},{6,10},{10,14},{3,7},{... | collective-permute-start | bytes 119816 | tf_op jit(solution)/shard_map/ppermute | solution.py:21
  78.3 0.7 gather_fusion
  79.0 1.0 collective-permute-done.3
  80.0 2.2 %fusion.47 = (f32[13,4,8,128]{3,0,2,1:T(8,128)S(1)}, f32[13,4,8,128]{3,0,2,1:T(8,128)S(1)}) fusion(f32[13]{0:T(128)S(1)} %gather_fusion, f32[4,8,128]{2,1,0:T(8,128)S(1)} %get-tuple-element.33, f32[13]{0:T(128)S(1)} %copy-done.6, f32[4,8,128]{2,1,0:T(8,128)S(1)} %get-tuple-element.31, f32[13,4,8,128]{3,0,2,1:T(8,128)} %all-reduce.8.cloned.1.call-done, ...), kind=kOutput, calls=%fused_computation.109 | convolution fusion | flops 9478144 | bytes 1522496 | tf_op jit(solution)/shard_map/cj,jxyz->cxyz/dot_general | solution.py:58
  82.2 1.3 collective-permute-start.4
  83.5 4.5 %collective-permute-start.5 = (f32[13,1,8,128]{3,0,2,1:T(8,128)S(1)}, f32[13,1,8,128]{3,0,2,1:T(8,128)S(1)}, u32[]{:S(2)}, u32[]{:S(2)}) collective-permute-start(f32[13,1,8,128]{3,0,2,1:T(8,128)S(1)} %get-tuple-element.27), channel_id=1, source_target_pairs={{0,16},{1,17},{2,18},{3,19},{4,20},{5,21},{6,22},{7,23},{8,24},{9,... | collective-permute-start | bytes 159752 | tf_op jit(solution)/shard_map/ppermute | solution.py:21
  88.0 0.3 collective-permute-done.4
  88.3 1.6 collective-permute-done.5
  89.9 1.3 collective-permute-start.6
  91.2 4.9 %collective-permute-start.7 = (f32[13,6,1,128]{3,0,2,1:T(8,128)S(1)}, f32[13,6,1,128]{3,0,2,1:T(8,128)S(1)}, u32[]{:S(2)}, u32[]{:S(2)}) collective-permute-start(f32[13,6,1,128]{3,0,2,1:T(8,128)S(1)} %get-tuple-element.16), channel_id=1, source_target_pairs={{0,4},{4,8},{8,12},{1,5},{5,9},{9,13},{2,6},{6,10},{10,14},{3,7},{... | collective-permute-start | bytes 119816 | tf_op jit(solution)/shard_map/ppermute | solution.py:21
  96.1 0.1 collective-permute-done.6
  96.2 1.6 collective-permute-done.7
  97.8 0.5 divide_add_fusion.2
  98.3 1.3 collective-permute-start.8
  99.6 4.5 %collective-permute-start.9 = (f32[13,1,8,128]{3,0,2,1:T(8,128)S(1)}, f32[13,1,8,128]{3,0,2,1:T(8,128)S(1)}, u32[]{:S(2)}, u32[]{:S(2)}) collective-permute-start(f32[13,1,8,128]{3,0,2,1:T(8,128)S(1)} %get-tuple-element.25), channel_id=1, source_target_pairs={{0,16},{1,17},{2,18},{3,19},{4,20},{5,21},{6,22},{7,23},{8,24},{9,... | collective-permute-start | bytes 159752 | tf_op jit(solution)/shard_map/ppermute | solution.py:21
  104.2 0.3 collective-permute-done.8
  104.5 1.6 collective-permute-done.9
  106.1 1.3 collective-permute-start.10
  107.4 4.9 %collective-permute-start.11 = (f32[13,6,1,128]{3,0,2,1:T(8,128)S(1)}, f32[13,6,1,128]{3,0,2,1:T(8,128)S(1)}, u32[]{:S(2)}, u32[]{:S(2)}) collective-permute-start(f32[13,6,1,128]{3,0,2,1:T(8,128)S(1)} %get-tuple-element.14), channel_id=1, source_target_pairs={{0,4},{4,8},{8,12},{1,5},{5,9},{9,13},{2,6},{6,10},{10,14},{3,7},{... | collective-permute-start | bytes 119816 | tf_op jit(solution)/shard_map/ppermute | solution.py:21
  112.3 0.1 collective-permute-done.10
  112.4 1.6 collective-permute-done.11
  114.0 0.5 divide_add_fusion.1
  114.5 1.3 collective-permute-start.12
  115.8 4.5 %collective-permute-start.13 = (f32[13,1,8,128]{3,0,2,1:T(8,128)S(1)}, f32[13,1,8,128]{3,0,2,1:T(8,128)S(1)}, u32[]{:S(2)}, u32[]{:S(2)}) collective-permute-start(f32[13,1,8,128]{3,0,2,1:T(8,128)S(1)} %get-tuple-element.23), channel_id=1, source_target_pairs={{0,16},{1,17},{2,18},{3,19},{4,20},{5,21},{6,22},{7,23},{8,24},{9,... | collective-permute-start | bytes 159752 | tf_op jit(solution)/shard_map/ppermute | solution.py:21
  120.3 0.3 collective-permute-done.12
  120.6 1.6 collective-permute-done.13
  122.2 1.3 collective-permute-start.14
  123.5 4.9 %collective-permute-start.15 = (f32[13,6,1,128]{3,0,2,1:T(8,128)S(1)}, f32[13,6,1,128]{3,0,2,1:T(8,128)S(1)}, u32[]{:S(2)}, u32[]{:S(2)}) collective-permute-start(f32[13,6,1,128]{3,0,2,1:T(8,128)S(1)} %get-tuple-element.12), channel_id=1, source_target_pairs={{0,4},{4,8},{8,12},{1,5},{5,9},{9,13},{2,6},{6,10},{10,14},{3,7},{... | collective-permute-start | bytes 119816 | tf_op jit(solution)/shard_map/ppermute | solution.py:21
  128.4 0.1 multiply_reduce_fusion.2
  128.5 0.1 multiply_reduce_fusion.1
  128.7 1.5 collective-permute-done.15
  130.1 0.5 broadcast_multiply_fusion
  130.7 0.1 copy.24
  130.8 1.3 collective-permute-start.16
  132.1 4.8 %collective-permute-start.17 = (f32[13,1,8,128]{3,0,2,1:T(8,128)S(1)}, f32[13,1,8,128]{3,0,2,1:T(8,128)S(1)}, u32[]{:S(2)}, u32[]{:S(2)}) collective-permute-start(f32[13,1,8,128]{3,0,2,1:T(8,128)S(1)} %get-tuple-element.21), channel_id=1, source_target_pairs={{0,16},{1,17},{2,18},{3,19},{4,20},{5,21},{6,22},{7,23},{8,24},{9,... | collective-permute-start | bytes 159752 | tf_op jit(solution)/shard_map/ppermute | solution.py:21
  136.9 0.2 copy.17
  137.0 0.0 slice-start
  137.0 5.7 %convolution_bitcast_fusion = f32[54,8,32,128]{3,1,2,0:T(8,128)S(1)} fusion(f32[13,4096]{1,0:T(8,128)S(1)} %bitcast.100, f32[432,13]{0,1:T(8,128)S(1)} %copy-done), kind=kOutput, calls=%fused_computation.5 | convolution fusion | flops 276037632 | bytes 7313344 | tf_op jit(solution)/shard_map/dot_general | solution.py:77
  142.8 0.0 slice-start.1
  142.8 4.4 %copy.18 = f32[54,8,32,128]{3,2,1,0:T(8,128)} copy(f32[54,8,32,128]{3,1,2,0:T(8,128)S(1)} %convolution_bitcast_fusion) | data formatting | bytes 14155776
  147.2 6.6 %add_convert_fusion = bf16[432,4,8,128]{3,2,1,0:T(8,128)(2,1)} fusion(f32[432,4,8,128]{3,2,1,0:T(8,128)S(1)} %bitcast.97, f32[432,4,8,128]{3,2,1,0:T(8,128)} %bitcast.99), kind=kLoop, calls=%fused_computation.4 | loop fusion | flops 3538944 | bytes 17694720 | tf_op jit(solution)/shard_map/convert_element_type | solution.py:78
  153.8 1.3 collective-permute-start.18
  155.1 4.9 %collective-permute-start.19 = (f32[13,6,1,128]{3,0,2,1:T(8,128)S(1)}, f32[13,6,1,128]{3,0,2,1:T(8,128)S(1)}, u32[]{:S(2)}, u32[]{:S(2)}) collective-permute-start(f32[13,6,1,128]{3,0,2,1:T(8,128)S(1)} %get-tuple-element.10), channel_id=1, source_target_pairs={{0,4},{4,8},{8,12},{1,5},{5,9},{9,13},{2,6},{6,10},{10,14},{3,7},{... | collective-permute-start | bytes 119816 | tf_op jit(solution)/shard_map/ppermute | solution.py:21
  159.9 0.4 fusion.2
  160.3 0.1 multiply_reduce_fusion
  160.4 1.2 collective-permute-done.19
  161.7 0.2 fusion.31
  161.9 0.2 fusion.50
  162.0 40.7 %all-reduce.5 = (f32[1,13]{1,0:T(1,128)S(1)}, f32[1,13]{1,0:T(1,128)S(1)}, f32[1,13]{1,0:T(1,128)S(1)}, f32[1,13]{1,0:T(1,128)S(1)}, f32[1,13]{1,0:T(1,128)S(1)}) all-reduce(f32[1,13]{1,0:T(1,128)S(1)} %bitcast.107, f32[1,13]{1,0:T(1,128)S(1)} %bitcast.103, ...), channel_id=1, replica_groups=mesh['cx'=2,'cyz'=4,'vert'=4] {'cx','cyz','vert'}, use_global_device_ids=true, to_apply=%region_2.3 | all-reduce | flops 65 | bytes 520 | tf_op jit(solution)/shard_map/psum | solution.py:43
  202.7 0.6 add_sqrt_fusion
  (37 shorter events, 0.2 us)
Async XLA Ops:
  7.2 129.9 %copy-start = (f32[432,13]{0,1:T(8,128)S(1)}, f32[432,13]{0,1:T(8,128)}, u32[]{:S(2)}) copy-start(f32[432,13]{0,1:T(8,128)} %param.11) | copy-start | bytes 67396
  7.2 54.7 %all-reduce.8.cloned.1.call-start = ((), (), s32[]{:S(2)}) async-start(), calls=%async_computation | async-start | bytes 524288 | tf_op jit(solution)/shard_map/psum | solution.py:52
  17.0 1.6 copy-start.3
  18.5 8.3 %copy-start.2 = (s32[4,8,128]{2,1,0:T(8,128)S(1)}, s32[4,8,128]{2,1,0:T(8,128)}, u32[]{:S(2)}) copy-start(s32[4,8,128]{2,1,0:T(8,128)} %param.9) | copy-start | bytes 49156
  18.5 59.7 %copy-start.1 = (f32[13,13]{1,0:T(8,128)S(1)}, f32[13,13]{1,0:T(8,128)}, u32[]{:S(2)}) copy-start(f32[13,13]{1,0:T(8,128)} %param.13) | copy-start | bytes 2032
  18.5 61.4 %copy-start.4 = (f32[13,13]{1,0:T(8,128)S(1)}, f32[13,13]{1,0:T(8,128)}, u32[]{:S(2)}) copy-start(f32[13,13]{1,0:T(8,128)} %param.12) | copy-start | bytes 2032
  18.5 61.4 %copy-start.5 = (f32[13]{0:T(128)S(1)}, f32[13]{0:T(128)}, u32[]{:S(2)}) copy-start(f32[13]{0:T(128)} %param.15) | copy-start | bytes 160
  18.6 61.4 %copy-start.6 = (f32[13]{0:T(128)S(1)}, f32[13]{0:T(128)}, u32[]{:S(2)}) copy-start(f32[13]{0:T(128)} %param.14) | copy-start | bytes 160
  62.8 5.3 %collective-permute-start.1 = (f32[13,1,8,128]{3,0,2,1:T(8,128)S(1)}, f32[13,1,8,128]{3,0,2,1:T(8,128)S(1)}, u32[]{:S(2)}, u32[]{:S(2)}) collective-permute-start(f32[13,1,8,128]{3,0,2,1:T(8,128)S(1)} %get-tuple-element.30), channel_id=1, source_target_pairs={{0,16},{1,17},{2,18},{3,19},{4,20},{5,21},{6,22},{7,23},{8,24},{9,... | collective-permute-start | bytes 159752 | tf_op jit(solution)/shard_map/ppermute | solution.py:21
  66.2 6.2 %collective-permute-start = (f32[13,1,8,128]{3,0,2,1:T(8,128)S(1)}, f32[13,1,8,128]{3,0,2,1:T(8,128)S(1)}, u32[]{:S(2)}, u32[]{:S(2)}) collective-permute-start(f32[13,1,8,128]{3,0,2,1:T(8,128)S(1)} %get-tuple-element.29), channel_id=1, source_target_pairs={{16,0},{17,1},{18,2},{19,3},{20,4},{21,5},{22,6},{23,7},{24,8},{25... | collective-permute-start | bytes 159752 | tf_op jit(solution)/shard_map/ppermute | solution.py:22
  72.4 6.6 %collective-permute-start.2 = (f32[13,6,1,128]{3,0,2,1:T(8,128)S(1)}, f32[13,6,1,128]{3,0,2,1:T(8,128)S(1)}, u32[]{:S(2)}, u32[]{:S(2)}) collective-permute-start(f32[13,6,1,128]{3,0,2,1:T(8,128)S(1)} %get-tuple-element.17), channel_id=1, source_target_pairs={{4,0},{8,4},{12,8},{5,1},{9,5},{13,9},{6,2},{10,6},{14,10},{7,3},{... | collective-permute-start | bytes 119816 | tf_op jit(solution)/shard_map/ppermute | solution.py:22
  73.7 6.3 %collective-permute-start.3 = (f32[13,6,1,128]{3,0,2,1:T(8,128)S(1)}, f32[13,6,1,128]{3,0,2,1:T(8,128)S(1)}, u32[]{:S(2)}, u32[]{:S(2)}) collective-permute-start(f32[13,6,1,128]{3,0,2,1:T(8,128)S(1)} %get-tuple-element.18), channel_id=1, source_target_pairs={{0,4},{4,8},{8,12},{1,5},{5,9},{9,13},{2,6},{6,10},{10,14},{3,7},{... | collective-permute-start | bytes 119816 | tf_op jit(solution)/shard_map/ppermute | solution.py:21
  82.2 6.2 %collective-permute-start.4 = (f32[13,1,8,128]{3,0,2,1:T(8,128)S(1)}, f32[13,1,8,128]{3,0,2,1:T(8,128)S(1)}, u32[]{:S(2)}, u32[]{:S(2)}) collective-permute-start(f32[13,1,8,128]{3,0,2,1:T(8,128)S(1)} %get-tuple-element.28), channel_id=1, source_target_pairs={{16,0},{17,1},{18,2},{19,3},{20,4},{21,5},{22,6},{23,7},{24,8},{25... | collective-permute-start | bytes 159752 | tf_op jit(solution)/shard_map/ppermute | solution.py:22
  83.5 6.4 %collective-permute-start.5 = (f32[13,1,8,128]{3,0,2,1:T(8,128)S(1)}, f32[13,1,8,128]{3,0,2,1:T(8,128)S(1)}, u32[]{:S(2)}, u32[]{:S(2)}) collective-permute-start(f32[13,1,8,128]{3,0,2,1:T(8,128)S(1)} %get-tuple-element.27), channel_id=1, source_target_pairs={{0,16},{1,17},{2,18},{3,19},{4,20},{5,21},{6,22},{7,23},{8,24},{9,... | collective-permute-start | bytes 159752 | tf_op jit(solution)/shard_map/ppermute | solution.py:21
  89.9 6.3 %collective-permute-start.6 = (f32[13,6,1,128]{3,0,2,1:T(8,128)S(1)}, f32[13,6,1,128]{3,0,2,1:T(8,128)S(1)}, u32[]{:S(2)}, u32[]{:S(2)}) collective-permute-start(f32[13,6,1,128]{3,0,2,1:T(8,128)S(1)} %get-tuple-element.15), channel_id=1, source_target_pairs={{4,0},{8,4},{12,8},{5,1},{9,5},{13,9},{6,2},{10,6},{14,10},{7,3},{... | collective-permute-start | bytes 119816 | tf_op jit(solution)/shard_map/ppermute | solution.py:22
  91.2 6.6 %collective-permute-start.7 = (f32[13,6,1,128]{3,0,2,1:T(8,128)S(1)}, f32[13,6,1,128]{3,0,2,1:T(8,128)S(1)}, u32[]{:S(2)}, u32[]{:S(2)}) collective-permute-start(f32[13,6,1,128]{3,0,2,1:T(8,128)S(1)} %get-tuple-element.16), channel_id=1, source_target_pairs={{0,4},{4,8},{8,12},{1,5},{5,9},{9,13},{2,6},{6,10},{10,14},{3,7},{... | collective-permute-start | bytes 119816 | tf_op jit(solution)/shard_map/ppermute | solution.py:21
  98.3 6.2 %collective-permute-start.8 = (f32[13,1,8,128]{3,0,2,1:T(8,128)S(1)}, f32[13,1,8,128]{3,0,2,1:T(8,128)S(1)}, u32[]{:S(2)}, u32[]{:S(2)}) collective-permute-start(f32[13,1,8,128]{3,0,2,1:T(8,128)S(1)} %get-tuple-element.26), channel_id=1, source_target_pairs={{16,0},{17,1},{18,2},{19,3},{20,4},{21,5},{22,6},{23,7},{24,8},{25... | collective-permute-start | bytes 159752 | tf_op jit(solution)/shard_map/ppermute | solution.py:22
  99.6 6.4 %collective-permute-start.9 = (f32[13,1,8,128]{3,0,2,1:T(8,128)S(1)}, f32[13,1,8,128]{3,0,2,1:T(8,128)S(1)}, u32[]{:S(2)}, u32[]{:S(2)}) collective-permute-start(f32[13,1,8,128]{3,0,2,1:T(8,128)S(1)} %get-tuple-element.25), channel_id=1, source_target_pairs={{0,16},{1,17},{2,18},{3,19},{4,20},{5,21},{6,22},{7,23},{8,24},{9,... | collective-permute-start | bytes 159752 | tf_op jit(solution)/shard_map/ppermute | solution.py:21
  106.1 6.3 %collective-permute-start.10 = (f32[13,6,1,128]{3,0,2,1:T(8,128)S(1)}, f32[13,6,1,128]{3,0,2,1:T(8,128)S(1)}, u32[]{:S(2)}, u32[]{:S(2)}) collective-permute-start(f32[13,6,1,128]{3,0,2,1:T(8,128)S(1)} %get-tuple-element.13), channel_id=1, source_target_pairs={{4,0},{8,4},{12,8},{5,1},{9,5},{13,9},{6,2},{10,6},{14,10},{7,3},{... | collective-permute-start | bytes 119816 | tf_op jit(solution)/shard_map/ppermute | solution.py:22
  107.4 6.6 %collective-permute-start.11 = (f32[13,6,1,128]{3,0,2,1:T(8,128)S(1)}, f32[13,6,1,128]{3,0,2,1:T(8,128)S(1)}, u32[]{:S(2)}, u32[]{:S(2)}) collective-permute-start(f32[13,6,1,128]{3,0,2,1:T(8,128)S(1)} %get-tuple-element.14), channel_id=1, source_target_pairs={{0,4},{4,8},{8,12},{1,5},{5,9},{9,13},{2,6},{6,10},{10,14},{3,7},{... | collective-permute-start | bytes 119816 | tf_op jit(solution)/shard_map/ppermute | solution.py:21
  114.5 6.2 %collective-permute-start.12 = (f32[13,1,8,128]{3,0,2,1:T(8,128)S(1)}, f32[13,1,8,128]{3,0,2,1:T(8,128)S(1)}, u32[]{:S(2)}, u32[]{:S(2)}) collective-permute-start(f32[13,1,8,128]{3,0,2,1:T(8,128)S(1)} %get-tuple-element.24), channel_id=1, source_target_pairs={{16,0},{17,1},{18,2},{19,3},{20,4},{21,5},{22,6},{23,7},{24,8},{25... | collective-permute-start | bytes 159752 | tf_op jit(solution)/shard_map/ppermute | solution.py:22
  115.8 6.4 %collective-permute-start.13 = (f32[13,1,8,128]{3,0,2,1:T(8,128)S(1)}, f32[13,1,8,128]{3,0,2,1:T(8,128)S(1)}, u32[]{:S(2)}, u32[]{:S(2)}) collective-permute-start(f32[13,1,8,128]{3,0,2,1:T(8,128)S(1)} %get-tuple-element.23), channel_id=1, source_target_pairs={{0,16},{1,17},{2,18},{3,19},{4,20},{5,21},{6,22},{7,23},{8,24},{9,... | collective-permute-start | bytes 159752 | tf_op jit(solution)/shard_map/ppermute | solution.py:21
  122.2 6.4 %collective-permute-start.14 = (f32[13,6,1,128]{3,0,2,1:T(8,128)S(1)}, f32[13,6,1,128]{3,0,2,1:T(8,128)S(1)}, u32[]{:S(2)}, u32[]{:S(2)}) collective-permute-start(f32[13,6,1,128]{3,0,2,1:T(8,128)S(1)} %get-tuple-element.11), channel_id=1, source_target_pairs={{4,0},{8,4},{12,8},{5,1},{9,5},{13,9},{6,2},{10,6},{14,10},{7,3},{... | collective-permute-start | bytes 119816 | tf_op jit(solution)/shard_map/ppermute | solution.py:22
  123.5 6.6 %collective-permute-start.15 = (f32[13,6,1,128]{3,0,2,1:T(8,128)S(1)}, f32[13,6,1,128]{3,0,2,1:T(8,128)S(1)}, u32[]{:S(2)}, u32[]{:S(2)}) collective-permute-start(f32[13,6,1,128]{3,0,2,1:T(8,128)S(1)} %get-tuple-element.12), channel_id=1, source_target_pairs={{0,4},{4,8},{8,12},{1,5},{5,9},{9,13},{2,6},{6,10},{10,14},{3,7},{... | collective-permute-start | bytes 119816 | tf_op jit(solution)/shard_map/ppermute | solution.py:21
  130.8 23.0 %collective-permute-start.16 = (f32[13,1,8,128]{3,0,2,1:T(8,128)S(1)}, f32[13,1,8,128]{3,0,2,1:T(8,128)S(1)}, u32[]{:S(2)}, u32[]{:S(2)}) collective-permute-start(f32[13,1,8,128]{3,0,2,1:T(8,128)S(1)} %get-tuple-element.22), channel_id=1, source_target_pairs={{16,0},{17,1},{18,2},{19,3},{20,4},{21,5},{22,6},{23,7},{24,8},{25... | collective-permute-start | bytes 159752 | tf_op jit(solution)/shard_map/ppermute | solution.py:22
  132.1 21.7 %collective-permute-start.17 = (f32[13,1,8,128]{3,0,2,1:T(8,128)S(1)}, f32[13,1,8,128]{3,0,2,1:T(8,128)S(1)}, u32[]{:S(2)}, u32[]{:S(2)}) collective-permute-start(f32[13,1,8,128]{3,0,2,1:T(8,128)S(1)} %get-tuple-element.21), channel_id=1, source_target_pairs={{0,16},{1,17},{2,18},{3,19},{4,20},{5,21},{6,22},{7,23},{8,24},{9,... | collective-permute-start | bytes 159752 | tf_op jit(solution)/shard_map/ppermute | solution.py:21
  137.0 10.1 %slice-start = ((s8[7077888]{0:T(1024)(128)(4,1)}), s8[4194304]{0:T(1024)(128)(4,1)S(1)}, s32[]{:S(2)}) async-start(s8[7077888]{0:T(1024)(128)(4,1)} %bitcast.96), calls=%async_computation.1 | async-start | bytes 8388608
  142.8 4.4 %slice-start.1 = ((s8[7077888]{0:T(1024)(128)(4,1)}), s8[2883584]{0:T(1024)(128)(4,1)S(1)}, s32[]{:S(2)}) async-start(s8[7077888]{0:T(1024)(128)(4,1)} %bitcast.96), calls=%async_computation.2 | async-start | bytes 5767168
  153.8 6.7 %collective-permute-start.18 = (f32[13,6,1,128]{3,0,2,1:T(8,128)S(1)}, f32[13,6,1,128]{3,0,2,1:T(8,128)S(1)}, u32[]{:S(2)}, u32[]{:S(2)}) collective-permute-start(f32[13,6,1,128]{3,0,2,1:T(8,128)S(1)} %get-tuple-element.9), channel_id=1, source_target_pairs={{4,0},{8,4},{12,8},{5,1},{9,5},{13,9},{6,2},{10,6},{14,10},{7,3},{... | collective-permute-start | bytes 119816 | tf_op jit(solution)/shard_map/ppermute | solution.py:22
  155.1 6.6 %collective-permute-start.19 = (f32[13,6,1,128]{3,0,2,1:T(8,128)S(1)}, f32[13,6,1,128]{3,0,2,1:T(8,128)S(1)}, u32[]{:S(2)}, u32[]{:S(2)}) collective-permute-start(f32[13,6,1,128]{3,0,2,1:T(8,128)S(1)} %get-tuple-element.10), channel_id=1, source_target_pairs={{0,4},{4,8},{8,12},{1,5},{5,9},{9,13},{2,6},{6,10},{10,14},{3,7},{... | collective-permute-start | bytes 119816 | tf_op jit(solution)/shard_map/ppermute | solution.py:21
Sparse Core Ops, SparseCore 0:
  26.9 34.9 all-reduce.7
where the time goes:
time: 211 us; the launch traced here: 210 us
  starting transfers between devices  58.8 us (28%)
  waiting for transfers between devices  51.9 us (25%)
  blocking collectives  40.7 us (19%)
  local copies, waits for them, and re-layouts  18.6 us (9%)
  matrix products  17.8 us (8%)
  between operations  14.5 us (7%)
  other arithmetic  7.97 us (4%)
    ppermute x10, starting transfers between devices, with_halo(): before = lax.ppermute(last, axis, up)  45.8 us
    psum x1, blocking collectives, summed_squares(): return lax.psum(local_sums, ('cx', 'cyz', 'vert'))  40.7 us
    psum x1, waiting for transfers between devices, local(): moments = lax.psum(partial_value, 'vert')  35.1 us
    unnamed x25, local copies, waits for them, and re-layouts  16.8 us
    ppermute x10, starting transfers between devices, with_halo(): after = lax.ppermute(leading, axis, down)  12.9 us
    ppermute x10, waiting for transfers between devices, with_halo(): before = lax.ppermute(last, axis, up)  12.2 us
    dot_general x1, matrix products, local(): jnp.dot(basis, dist.reshape(vel_local, -1), precision=highest)  8.16 us
    convert_element_type x1, other arithmetic, local(): new_dist = (dist + delta.reshape(dist.shape)).astype(jnp.bfloat16)  6.58 us
  transfers between devices with their start and end apart: 21, of which 16 were waited for; matrix products, arithmetic and copies ran while one was open for 9% of the time, Pallas kernels for 0%

commit v1 on v0

v1 whole, which is shorter than its diff:
```python
import functools
import math

import jax
import jax.numpy as jnp
from jax import lax
from jax.experimental import pallas as pl
from jax.experimental.pallas import tpu as pltpu
from jax.sharding import PartitionSpec as P

ITERS = 4
PAD = 16
CHUNKS = 3
MESH = pl.DeviceIdType.MESH
f32 = jnp.float32
bf16 = jnp.bfloat16


def halves(x):
    high = x.astype(bf16)
    return high, (x - high.astype(f32)).astype(bf16)


def kernel(
    sizes, dist, cell_type, basis, backmap, source_map, coupling, diffusivity, gain,
    out, norms,
    dist_v, out_v, delta_v, cells_v, basis_v, wide_v, back_v, backw_v, backs_v,
    part, arrived, field, xh, ystage, yh, planes_v, sq, first, second,
    dist_sem, small_sem, rs_s, rs_r, h_s, h_r, ag_s, ag_r, a1_s, a1_r, a2_s, a2_r, out_sem,
):
    ncx, ncyz, nv, fields, vel, rows, lanes = sizes
    cx, cyz, me = lax.axis_index("cx"), lax.axis_index("cyz"), lax.axis_index("vert")

    def at(c, y, v):
        return {"cx": c, "cyz": y, "vert": v}

    odd = cx % 2

    def plane_of(v):
        return v + odd * (nv - 1 - 2 * v)

    chip, core = me // 2, me % 2
    order = []
    for da in list(range(1, nv // 2)) + [0]:
        for db in (0, 1) if da else (1, 0):
            order.append(2 * ((chip + da) % (nv // 2)) + (core + db) % 2)
    last = nv - 1

    loads = []
    for step, owner in enumerate(order):
        copy = pltpu.make_async_copy(
            dist.at[:, plane_of(owner)], dist_v.at[step], dist_sem.at[step]
        )
        copy.start()
        loads.append(copy)
        if step == 0:
            get_basis = pltpu.make_async_copy(basis, basis_v, small_sem.at[0])
            get_basis.start()
    get_back = pltpu.make_async_copy(backmap, back_v, small_sem.at[1])
    get_cells = pltpu.make_async_copy(cell_type, cells_v, small_sem.at[2])
    get_back.start()
    get_cells.start()

    group = [
        (dx, dv) for dx in range(ncx) for dv in range(nv) if (dx, dv) != (0, 0)
    ]
    barrier = pltpu.get_barrier_semaphore()
    for dx, dv in group:
        pl.semaphore_signal(
            barrier, inc=1, device_id=at((cx + dx) % ncx, cyz, (me + dv) % nv), device_id_type=MESH
        )
    for dy in range(1, ncyz):
        pl.semaphore_signal(
            barrier, inc=1, device_id=at(cx, (cyz + dy) % ncyz, me), device_id_type=MESH
        )

    spot = plane_of(me)
    low, high = spot == 0, spot == nv - 1
    side = 1 - 2 * odd
    left = at(jnp.where(low, cx - 1, cx), cyz, jnp.where(low, me, me - side))
    right = at(jnp.where(high, cx + 1, cx), cyz, jnp.where(high, me, me + side))
    prev, following = at(cx, cyz - 1, me), at(cx, cyz + 1, me)
    place = cx * nv + spot
    has = [place > 0, place < ncx * nv - 1, cyz > 0, cyz < ncyz - 1]
    to = [left, right, prev, following]

    sq[...] = jnp.zeros_like(sq)
    planes_v[...] = jnp.zeros_like(planes_v)
    wide_v[...] = jnp.zeros_like(wide_v)
    for direction in range(2):

        @pl.when(jnp.logical_not(has[direction]))
        def _():
            for k in range(ITERS + 1):
                xh[k, direction] = jnp.zeros((fields * rows, lanes), f32)

        @pl.when(jnp.logical_not(has[2 + direction]))
        def _():
            for k in range(ITERS + 1):
                yh[k, direction] = jnp.zeros((fields, lanes), f32)

    get_basis.wait()
    wide_v[0:fields, :] = basis_v[...]
    weights = jnp.concatenate(halves(wide_v[...]), axis=0)

    def remote(src, dst, send, recv, device):
        return pltpu.make_async_remote_copy(
            src_ref=src, dst_ref=dst, send_sem=send, recv_sem=recv,
            device_id=device, device_id_type=MESH,
        )

    used = pl.ds(0, fields * rows)

    def scatter(owner, source):
        return remote(
            part.at[owner, used], arrived.at[source], rs_s.at[owner], rs_r.at[source],
            at(cx, cyz, owner),
        )

    for step, owner in enumerate(order):
        loads[step].wait()
        flat = dist_v.at[step].reshape(vel * rows, lanes)
        for y in range(0, rows, 2):
            pair = jnp.concatenate(
                [flat[pl.ds(y + i, vel, stride=rows), :] for i in range(2)], axis=1
            )
            top, rest = halves(pair)
            both = jnp.dot(weights, top, preferred_element_type=f32) + jnp.dot(
                weights, rest, preferred_element_type=f32
            )
            both = both[0:PAD] + both[PAD:]
            for i in range(2):
                part[owner, pl.ds(y + i, PAD, stride=rows), :] = both[:, i * lanes:(i + 1) * lanes]
        if step == 0:
            pl.semaphore_wait(barrier, len(group) + ncyz - 1)
        if step < last:
            scatter(owner, me).start()

    get_cells.wait()
    kinds = cells_v[spot]
    fluid = jnp.where(kinds == 0, 1.0, 0.0).astype(f32)
    inlet = jnp.where(kinds == 2, 1.0, 0.0).astype(f32)
    outlet = jnp.where(kinds == 3, 1.0, 0.0).astype(f32)
    active = fluid + outlet
    row = lax.broadcasted_iota(jnp.int32, (rows, lanes), 0)
    lane = lax.broadcasted_iota(jnp.int32, (rows, lanes), 1)

    def tile(c):
        return pl.ds(c * rows, rows)

    def mix(matrix, w):
        mixed = []
        for c in range(fields):
            total = matrix[c, 0] * w[0]
            for j in range(1, fields):
                total = total + matrix[c, j] * w[j]
            mixed.append(total)
        return mixed

    def halo(k, d):
        if d < 2:
            return remote(field.at[k], xh.at[k, 1 - d], h_s.at[k, d], h_r.at[k, 1 - d], to[d])
        return remote(
            ystage.at[k, d - 2], yh.at[k, 3 - d], h_s.at[k, d], h_r.at[k, 5 - d], to[d]
        )

    def landed(k, d):
        if d < 2:
            return remote(field.at[k], xh.at[k, d], h_s.at[k, d], h_r.at[k, d], to[d])
        return remote(ystage.at[k, d - 2], yh.at[k, d - 2], h_s.at[k, d], h_r.at[k, d], to[d])

    def start_halo(k, w):
        for c in range(fields):
            field[k, tile(c), :] = w[c]
            ystage[k, 0, pl.ds(c, 1), :] = w[c][0:1]
            ystage[k, 1, pl.ds(c, 1), :] = w[c][rows - 1:rows]
        for d in range(4):

            @pl.when(has[d])
            def _():
                halo(k, d).start()

    def wait_halo(k):
        for d in range(4):

            @pl.when(has[d])
            def _():
                landed(k, d).wait_recv()

    def laplace(k, w):
        result = []
        for c in range(fields):
            x = w[c]
            near = xh[k, 0, tile(c), :] + xh[k, 1, tile(c), :]
            above = jnp.broadcast_to(yh[k, 0, pl.ds(c, 1), :], (rows, lanes))
            below = jnp.broadcast_to(yh[k, 1, pl.ds(c, 1), :], (rows, lanes))
            near = near + jnp.where(row == 0, above, pltpu.roll(x, 1, 0))
            near = near + jnp.where(row == rows - 1, below, pltpu.roll(x, rows - 1, 0))
            near = near + jnp.where(lane == 0, 0.0, pltpu.roll(x, 1, 1))
            near = near + jnp.where(lane == lanes - 1, 0.0, pltpu.roll(x, lanes - 1, 1))
            result.append(6.0 * x - near)
        return result

    def keep_squares(k, r):
        for c in range(fields):
            sq[pl.ds(k * fields + c, 1), :] = jnp.sum(r[c] * r[c], axis=0, keepdims=True)

    for owner in order[:-1]:
        scatter(owner, owner).wait_recv()
    moments = []
    for c in range(fields):
        total = part[me, tile(c), :]
        for owner in order[:-1]:
            total = total + arrived[owner, tile(c), :]
        moments.append(total)

    start_halo(0, moments)
    mixed = mix(source_map, moments)
    inverse = [
        1.0 / (1.0 + 6.0 * active * diffusivity[c] - fluid * coupling[c, c])
        for c in range(fields)
    ]
    get_back.wait()
    backw_v[...] = jnp.zeros_like(backw_v)
    backw_v[:, 0:fields] = back_v[...]
    wide = backw_v[...]
    top = wide.astype(bf16).astype(f32)
    rest = wide - top
    backs_v[...] = (
        top + pltpu.roll(top, PAD, 1) + pltpu.roll(rest, 2 * PAD, 1) + pltpu.roll(rest, 3 * PAD, 1)
    ).astype(bf16)
    wait_halo(0)
    bent = laplace(0, moments)
    target = [
        active * (mixed[c] - gain[c] * bent[c]) + inlet * moments[c] for c in range(fields)
    ]

    def omega(k):
        return 1.0 / (1.0 + 0.8 * math.cos(math.pi * (2 * k + 1) / (2 * ITERS)))

    def residual(k, w, coupled):
        bent = laplace(k, w)
        return [
            target[c] - (w[c] + active * diffusivity[c] * bent[c] - fluid * coupled[c])
            for c in range(fields)
        ]

    correction = [omega(0) * target[c] * inverse[c] for c in range(fields)]
    resid = target
    for k in range(1, ITERS):
        start_halo(k, correction)
        keep_squares(k - 1, resid)
        coupled = mix(coupling, correction)
        wait_halo(k)
        resid = residual(k, correction, coupled)
        correction = [
            correction[c] + omega(k) * resid[c] * inverse[c] for c in range(fields)
        ]
    start_halo(ITERS, correction)
    for c in range(fields):
        planes_v[me, tile(c), :] = correction[c]

    def gather(source, peer):
        return remote(
            planes_v.at[source, used], planes_v.at[source, used], ag_s.at[peer], ag_r.at[source],
            at(cx, cyz, peer),
        )

    for owner in order[:-1]:
        gather(me, owner).start()
    keep_squares(ITERS - 1, resid)
    coupled = mix(coupling, correction)

    size = vel // CHUNKS
    stores = []

    def finish(step):
        owner = order[step]
        if step < last:
            gather(owner, owner).wait_recv()
        columns = jnp.concatenate(
            [planes_v[owner, pl.ds(y, PAD, stride=rows), :] for y in range(rows)], axis=1
        )
        top, rest = halves(columns)
        stacked = jnp.concatenate(
            [top, rest, top, rest, jnp.zeros((lanes - 4 * PAD, rows * lanes), bf16)], axis=0
        )
        for chunk in range(CHUNKS):
            span = pl.ds(chunk * size, size)
            flat = delta_v.at[chunk].reshape(size * rows, lanes)
            for y in range(0, rows, 2):
                delta = jnp.dot(
                    backs_v[span, :], stacked[:, y * lanes:(y + 2) * lanes],
                    preferred_element_type=f32,
                )
                for i in range(2):
                    flat[pl.ds(y + i, size, stride=rows), :] = delta[:, i * lanes:(i + 1) * lanes]
            out_v[step, span] = (dist_v[step, span] + delta_v[chunk]).astype(bf16)
        copy = pltpu.make_async_copy(out_v.at[step], out.at[:, plane_of(owner)], out_sem.at[step])
        copy.start()
        stores.append(copy)

    finish(last)
    wait_halo(ITERS)
    keep_squares(ITERS, residual(ITERS, correction, coupled))
    mine = cx * nv + me
    first[mine] = lax.dot_general(
        jnp.ones((rows, lanes), f32), sq[...], (((1,), (1,)), ((), ())),
        precision=lax.Precision.HIGHEST, preferred_element_type=f32,
    )

    def sum_first(slot, index, c, v):
        return remote(first.at[slot], first.at[slot], a1_s.at[index], a1_r.at[slot], at(c, cyz, v))

    def sum_second(slot, index, y):
        return remote(second.at[slot], second.at[slot], a2_s.at[index], a2_r.at[slot], at(cx, y, me))

    for index, (dx, dv) in enumerate(group):
        sum_first(mine, index, (cx + dx) % ncx, (me + dv) % nv).start()
    finish(last - 1)
    for index, (dx, dv) in enumerate(group):
        c, v = (cx + dx) % ncx, (me + dv) % nv
        sum_first(c * nv + v, index, c, v).wait_recv()
    total = first[0]
    for i in range(1, ncx * nv):
        total = total + first[i]
    second[cyz] = total
    for dy in range(1, ncyz):
        sum_second(cyz, dy, (cyz + dy) % ncyz).start()
    for step in range(last - 2, -1, -1):
        finish(step)
    for dy in range(1, ncyz):
        y = (cyz + dy) % ncyz
        sum_second(y, dy, y).wait_recv()
    total = second[0]
    for i in range(1, ncyz):
        total = total + second[i]
    value = jnp.sqrt(total / (ncx * nv * rows * ncyz * lanes) + 1e-06)
    for k in range(ITERS + 1):
        shifted = value if k == 0 else pltpu.roll(value, lanes - k * fields, 1)
        norms[pl.ds(k, 1), :] = shifted[0:1, 0:fields]

    for owner in order[:-1]:
        scatter(owner, me).wait_send()
        gather(me, owner).wait_send()
    for k in range(ITERS + 1):
        for d in range(4):

            @pl.when(has[d])
            def _():
                halo(k, d).wait_send()

    for index, (dx, dv) in enumerate(group):
        sum_first(mine, index, (cx + dx) % ncx, (me + dv) % nv).wait_send()
    for dy in range(1, ncyz):
        sum_second(cyz, dy, (cyz + dy) % ncyz).wait_send()
    for copy in stores:
        copy.wait()


def local(mesh_shape, *args):
    dist, cell_type, basis = args[:3]
    ncx, ncyz, nv = mesh_shape
    vel, planes, rows, lanes = dist.shape
    fields = basis.shape[0]
    assert planes == nv and nv % 2 == 0 and vel % (CHUNKS * 16) == 0
    sizes = (ncx, ncyz, nv, fields, vel, rows, lanes)
    anywhere = pl.BlockSpec(memory_space=pl.ANY)
    scalars = pl.BlockSpec(memory_space=pltpu.SMEM)
    rounds = ITERS + 1
    dma = pltpu.SemaphoreType.DMA
    deep = fields * rows
    return pl.pallas_call(
        functools.partial(kernel, sizes),
        out_shape=(
            jax.ShapeDtypeStruct(dist.shape, bf16),
            jax.ShapeDtypeStruct((rounds, fields), f32),
        ),
        in_specs=[anywhere] * 4 + [scalars] * 4,
        out_specs=(anywhere, pl.BlockSpec(memory_space=pltpu.VMEM)),
        scratch_shapes=[
            pltpu.VMEM((nv, vel, rows, lanes), f32),
            pltpu.VMEM((nv, vel, rows, lanes), bf16),
            pltpu.VMEM((CHUNKS, vel // CHUNKS, rows, lanes), f32),
            pltpu.VMEM(cell_type.shape, jnp.int32),
            pltpu.VMEM((fields, vel), f32),
            pltpu.VMEM((PAD, vel), f32),
            pltpu.VMEM((vel, fields), f32),
            pltpu.VMEM((vel, lanes), f32),
            pltpu.VMEM((vel, lanes), bf16),
            pltpu.VMEM((nv, PAD * rows, lanes), f32),
            pltpu.VMEM((nv, deep, lanes), f32),
            pltpu.VMEM((rounds, deep, lanes), f32),
            pltpu.VMEM((rounds, 2, deep, lanes), f32),
            pltpu.VMEM((rounds, 2, fields, lanes), f32),
            pltpu.VMEM((rounds, 2, fields, lanes), f32),
            pltpu.VMEM((nv, PAD * rows, lanes), f32),
            pltpu.VMEM((lanes, lanes), f32),
            pltpu.VMEM((ncx * nv, rows, lanes), f32),
            pltpu.VMEM((ncyz, rows, lanes), f32),
            dma((nv,)), dma((3,)), dma((nv,)), dma((nv,)),
            dma((rounds, 4)), dma((rounds, 4)), dma((nv,)), dma((nv,)),
            dma((ncx * nv,)), dma((ncx * nv,)), dma((ncyz,)), dma((ncyz,)), dma((nv,)),
        ],
        compiler_params=pltpu.CompilerParams(
            collective_id=0, has_side_effects=True, vmem_limit_bytes=40 * 2**20
        ),
    )(*args)


def solution(mesh):
    placed = (
        P("vert", "cx", "cyz", None),
        P("cx", "cyz", None),
        P(None, "vert"),
        P("vert", None),
        P(),
        P(),
        P(),
        P(),
    )
    shape = tuple(mesh.shape[name] for name in ("cx", "cyz", "vert"))
    return jax.shard_map(
        functools.partial(local, shape),
        mesh=mesh,
        in_specs=placed,
        out_specs=(P("vert", "cx", "cyz", None), P()),
        check_vma=False,
    )
```

time: 211 us -> 44.9 us (0.21)
  starting transfers between devices: 58.8 us -> 0 us
  waiting for transfers between devices: 51.9 us -> 0 us
  blocking collectives: 40.7 us -> 0 us
  Pallas kernels: 0 us -> 33.3 us
  matrix products: 17.8 us -> 0 us
  between operations: 14.5 us -> 0.66 us
  local copies, waits for them, and re-layouts: 18.6 us -> 10.5 us
  other arithmetic: 7.97 us -> 0 us
    ppermute x20 -> x0, starting transfers between devices: 58.8 us -> none  [the longest x10 45.8 us: with_halo(): before = lax.ppermute(last, axis, up)]
    psum x1 -> x0, blocking collectives: 40.7 us -> none  [summed_squares(): return lax.psum(local_sums, ('cx', 'cyz', 'vert'))]
    psum x1 -> x0, waiting for transfers between devices: 35.1 us -> none  [local(): moments = lax.psum(partial_value, 'vert')]
    pallas_call x0 -> x1, Pallas kernels: none -> 33.3 us  [local(): pl.pallas_call(functools.partial(kernel, sizes), out_shape=(jax.ShapeDtyp...]
    dot_general x7 -> x0, matrix products: 17.8 us -> none  [the longest x1 8.16 us: local(): jnp.dot(basis, dist.reshape(vel_local, -1), precision=highest)]
    ppermute x20 -> x0, waiting for transfers between devices: 16.7 us -> none  [the longest x10 12.2 us: with_halo(): before = lax.ppermute(last, axis, up)]
    convert_element_type x2 -> x0, other arithmetic: 6.58 us -> none  [the longest x1 6.58 us: local(): new_dist = (dist + delta.reshape(dist.shape)).astype(jnp.bfloat16)]
    unnamed x25 -> x17, local copies, waits for them, and re-layouts: 16.8 us -> 10.5 us
  transfers between devices with their start and end apart: 21 -> 0, of which waited for: 16 -> 0; matrix products, arithmetic and copies ran while one was open for 9% -> 0% of each run, Pallas kernels for 0% -> 0%
where the time goes in v1:
time: 44.9 us; the launch traced here: 44.4 us
  Pallas kernels  33.3 us (74%)
  local copies, waits for them, and re-layouts  10.5 us (23%)
  between operations  0.66 us (1%)
    pallas_call x1, Pallas kernels, local(): pl.pallas_call(functools.partial(kernel, sizes), out_shape=(jax.ShapeDtyp...  33.3 us
    unnamed x17, local copies, waits for them, and re-layouts  10.5 us

profile of v1, /device:TPU:0, one launch (start us, length us, event | category | flops | bytes accessed | tf_op | source)
XLA Modules:
  0.0 44.4 jit_solution(5577804911085539842)
XLA Ops:
  0.6 0.9 %copy.10.backmap = f32[432,13]{1,0:T(8,128)S(1)} copy(f32[432,13]{0,1:T(8,128)} %param.11) | data formatting | bytes 44928 | tf_op args[3]
  1.5 0.0 copy-start
  1.5 3.0 %copy-done = f32[432,4,8,128]{3,2,1,0:T(8,128)S(1)} copy-done((f32[432,4,8,128]{3,2,1,0:T(8,128)S(1)}, f32[432,4,8,128]{3,2,1,0:T(8,128)}, u32[]{:S(2)}) %copy-start) | copy-done | bytes 7077912
  4.5 0.0 copy-start.1
  4.5 0.8 %copy-done.1 = f32[13,432]{1,0:T(8,128)S(1)} copy-done((f32[13,432]{1,0:T(8,128)S(1)}, f32[13,432]{1,0:T(8,128)}, u32[]{:S(2)}) %copy-start.1) | copy-done | bytes 22488
  5.3 0.0 copy-start.2
  5.3 0.7 %copy-done.2 = s32[4,8,128]{2,1,0:T(8,128)S(1)} copy-done((s32[4,8,128]{2,1,0:T(8,128)S(1)}, s32[4,8,128]{2,1,0:T(8,128)}, u32[]{:S(2)}) %copy-start.2) | copy-done | bytes 16408
  6.0 0.0 copy-start.3
  6.0 0.7 %copy-done.3 = f32[13,13]{1,0:T(8,128)S(1)} copy-done((f32[13,13]{1,0:T(8,128)S(1)}, f32[13,13]{1,0:T(8,128)}, u32[]{:S(2)}) %copy-start.3) | copy-done | bytes 700
  6.7 0.0 copy-start.4
  6.7 0.7 %copy-done.4 = f32[13,13]{1,0:T(8,128)S(1)} copy-done((f32[13,13]{1,0:T(8,128)S(1)}, f32[13,13]{1,0:T(8,128)}, u32[]{:S(2)}) %copy-start.4) | copy-done | bytes 700
  7.4 0.0 copy-start.5
  7.4 0.7 %copy-done.5 = f32[13]{0:T(128)S(1)} copy-done((f32[13]{0:T(128)S(1)}, f32[13]{0:T(128)}, u32[]{:S(2)}) %copy-start.5) | copy-done | bytes 76
  8.1 0.0 copy-start.6
  8.1 0.7 %copy-done.6 = f32[13]{0:T(128)S(1)} copy-done((f32[13]{0:T(128)S(1)}, f32[13]{0:T(128)}, u32[]{:S(2)}) %copy-start.6) | copy-done | bytes 76
  8.7 33.3 %shard_map.95 = (bf16[432,4,8,128]{3,2,1,0:T(8,128)(2,1)S(1)}, f32[5,13]{1,0:T(8,128)S(1)}) custom-call(f32[432,4,8,128]{3,2,1,0:T(8,128)S(1)} %copy-done, s32[4,8,128]{2,1,0:T(8,128)S(1)} %copy-done.2, f32[13,432]{1,0:T(8,128)S(1)} %copy-done.1, f32[432,13]{1,0:T(8,128)S(1)} %copy.10.backmap, f32[13,13]{1,0:T(8,128)S(1)} %copy-done.3, ...), custom_call_target="tpu_custom_call" | custom-call | tf_op jit(solution)/shard_map/pallas_call | solution.py:373
  42.0 1.8 %copy.13 = bf16[432,4,8,128]{3,2,1,0:T(8,128)(2,1)} copy(bf16[432,4,8,128]{3,2,1,0:T(8,128)(2,1)S(1)} %get-tuple-element.4) | data formatting | bytes 7077888
  43.8 0.6 %copy.14 = f32[5,13]{1,0:T(8,128)} copy(f32[5,13]{1,0:T(8,128)S(1)} %get-tuple-element.5) | data formatting | bytes 520
Async XLA Ops:
  1.5 3.0 %copy-start = (f32[432,4,8,128]{3,2,1,0:T(8,128)S(1)}, f32[432,4,8,128]{3,2,1,0:T(8,128)}, u32[]{:S(2)}) copy-start(f32[432,4,8,128]{3,2,1,0:T(8,128)} %dist.1) | copy-start | bytes 21233668
  4.5 0.8 %copy-start.1 = (f32[13,432]{1,0:T(8,128)S(1)}, f32[13,432]{1,0:T(8,128)}, u32[]{:S(2)}) copy-start(f32[13,432]{1,0:T(8,128)} %basis.1) | copy-start | bytes 67396
  5.3 0.7 %copy-start.2 = (s32[4,8,128]{2,1,0:T(8,128)S(1)}, s32[4,8,128]{2,1,0:T(8,128)}, u32[]{:S(2)}) copy-start(s32[4,8,128]{2,1,0:T(8,128)} %cell_type.1) | copy-start | bytes 49156
  6.0 0.7 %copy-start.3 = (f32[13,13]{1,0:T(8,128)S(1)}, f32[13,13]{1,0:T(8,128)}, u32[]{:S(2)}) copy-start(f32[13,13]{1,0:T(8,128)} %source_map.1) | copy-start | bytes 2032
  6.7 0.7 %copy-start.4 = (f32[13,13]{1,0:T(8,128)S(1)}, f32[13,13]{1,0:T(8,128)}, u32[]{:S(2)}) copy-start(f32[13,13]{1,0:T(8,128)} %coupling.1) | copy-start | bytes 2032
  7.4 0.7 %copy-start.5 = (f32[13]{0:T(128)S(1)}, f32[13]{0:T(128)}, u32[]{:S(2)}) copy-start(f32[13]{0:T(128)} %diffusivity.1) | copy-start | bytes 160
  8.1 0.7 %copy-start.6 = (f32[13]{0:T(128)S(1)}, f32[13]{0:T(128)}, u32[]{:S(2)}) copy-start(f32[13]{0:T(128)} %gain.1) | copy-start | bytes 160

commit v2 on v1

--- a/solution.py
+++ b/solution.py
@@ -222,13 +222,14 @@
     ]
     get_back.wait()
     backw_v[...] = jnp.zeros_like(backw_v)
-    backw_v[:, 0:fields] = back_v[...]
+    backw_v[0:fields, 0:vel] = back_v[...]
     wide = backw_v[...]
     top = wide.astype(bf16).astype(f32)
     rest = wide - top
-    backs_v[...] = (
-        top + pltpu.roll(top, PAD, 1) + pltpu.roll(rest, 2 * PAD, 1) + pltpu.roll(rest, 3 * PAD, 1)
-    ).astype(bf16)
+    turned = jnp.concatenate(
+        [top, top, rest, rest, jnp.zeros((lanes - 4 * PAD, wide.shape[1]), f32)], axis=0
+    ).T
+    backs_v[...] = turned[0:vel].astype(bf16)
     wait_halo(0)
     bent = laplace(0, moments)
     target = [
@@ -385,8 +386,8 @@
             pltpu.VMEM(cell_type.shape, jnp.int32),
             pltpu.VMEM((fields, vel), f32),
             pltpu.VMEM((PAD, vel), f32),
-            pltpu.VMEM((vel, fields), f32),
-            pltpu.VMEM((vel, lanes), f32),
+            pltpu.VMEM((fields, vel), f32),
+            pltpu.VMEM((PAD, -(-vel // lanes) * lanes), f32),
             pltpu.VMEM((vel, lanes), bf16),
             pltpu.VMEM((nv, PAD * rows, lanes), f32),
             pltpu.VMEM((nv, deep, lanes), f32),
@@ -403,9 +404,9 @@
             dma((ncx * nv,)), dma((ncx * nv,)), dma((ncyz,)), dma((ncyz,)), dma((nv,)),
         ],
         compiler_params=pltpu.CompilerParams(
-            collective_id=0, has_side_effects=True, vmem_limit_bytes=40 * 2**20
+            collective_id=0, has_side_effects=True, vmem_limit_bytes=67043328
         ),
-    )(*args)
+    )(*args[:3], args[3].T, *args[4:])
 
 
 def solution(mesh):

time: 44.9 us -> 39.5 us (0.88)
  local copies, waits for them, and re-layouts: 10.5 us -> 5 us
    unnamed x17 -> x4, local copies, waits for them, and re-layouts: 10.5 us -> 5 us
where the time goes in v2:
time: 39.5 us; the launch traced here: 39.3 us
  Pallas kernels  33.7 us (85%)
  local copies, waits for them, and re-layouts  5 us (13%)
  between operations  0.65 us (2%)
    pallas_call x1, Pallas kernels, local(): pl.pallas_call(functools.partial(kernel, sizes), out_shape=(jax.ShapeDtyp...  33.7 us
    unnamed x4, local copies, waits for them, and re-layouts  5 us

profile of v2, /device:TPU:0, one launch (start us, length us, event | category | flops | bytes accessed | tf_op | source)
XLA Modules:
  0.0 39.3 jit_solution(9792674144616844925)
XLA Ops:
  0.6 33.7 %shard_map.95 = (bf16[432,4,8,128]{3,2,1,0:T(8,128)(2,1)}, f32[5,13]{1,0:T(8,128)}) custom-call(f32[432,4,8,128]{3,2,1,0:T(8,128)} %dist.1, s32[4,8,128]{2,1,0:T(8,128)} %cell_type.1, f32[13,432]{1,0:T(8,128)} %basis.1, f32[13,432]{1,0:T(8,128)} %bitcast.1, f32[13,13]{1,0:T(8,128)} %source_map.1, f32[13,13]{1,0:T(8,128)} %coupling.1, f32[13]{0:T(128)} %diffusivity.1, ...), custom_call_target="tpu_custom_call" | custom-call | tf_op jit(solution)/shard_map/pallas_call | solution.py:374
  34.3 0.0 copy-start
  34.3 4.4 %copy.12 = bf16[432,4,8,128]{3,2,1,0:T(8,128)(2,1)} copy(bf16[432,4,8,128]{3,2,1,0:T(8,128)(2,1)} %get-tuple-element.4) | data formatting | bytes 7077888
  38.7 0.0 copy-done
  38.7 0.6 %copy.13 = f32[5,13]{1,0:T(8,128)} copy(f32[5,13]{1,0:T(8,128)S(1)} %copy-done) | data formatting | bytes 520
Async XLA Ops:
  34.3 4.4 %copy-start = (f32[5,13]{1,0:T(8,128)S(1)}, f32[5,13]{1,0:T(8,128)}, u32[]{:S(2)}) copy-start(f32[5,13]{1,0:T(8,128)} %get-tuple-element.5) | copy-start | bytes 784

commit v3 on v2

--- a/solution.py
+++ b/solution.py
@@ -22,9 +22,9 @@
 
 
 def kernel(
-    sizes, dist, cell_type, basis, backmap, source_map, coupling, diffusivity, gain,
+    sizes, dist, cell_type, basis, backmap, source_hbm, coupling_hbm, diffusivity_hbm, gain_hbm,
     out, norms,
-    dist_v, out_v, delta_v, cells_v, basis_v, wide_v, back_v, backw_v, backs_v,
+    source_map, coupling, diffusivity, gain, dist_v, out_v, delta_v, cells_v, basis_v, wide_v, back_v, backw_v, backs_v,
     part, arrived, field, xh, ystage, yh, planes_v, sq, first, second,
     dist_sem, small_sem, rs_s, rs_r, h_s, h_r, ag_s, ag_r, a1_s, a1_r, a2_s, a2_r, out_sem,
 ):
@@ -60,6 +60,15 @@
     get_cells = pltpu.make_async_copy(cell_type, cells_v, small_sem.at[2])
     get_back.start()
     get_cells.start()
+    scalars = [
+        pltpu.make_async_copy(a, b, small_sem.at[3 + i])
+        for i, (a, b) in enumerate((
+            (source_hbm, source_map), (coupling_hbm, coupling),
+            (diffusivity_hbm, diffusivity), (gain_hbm, gain),
+        ))
+    ]
+    for copy in scalars:
+        copy.start()
 
     group = [
         (dx, dv) for dx in range(ncx) for dv in range(nv) if (dx, dv) != (0, 0)
@@ -137,6 +146,8 @@
             scatter(owner, me).start()
 
     get_cells.wait()
+    for copy in scalars:
+        copy.wait()
     kinds = cells_v[spot]
     fluid = jnp.where(kinds == 0, 1.0, 0.0).astype(f32)
     inlet = jnp.where(kinds == 2, 1.0, 0.0).astype(f32)
@@ -367,7 +378,7 @@
     assert planes == nv and nv % 2 == 0 and vel % (CHUNKS * 16) == 0
     sizes = (ncx, ncyz, nv, fields, vel, rows, lanes)
     anywhere = pl.BlockSpec(memory_space=pl.ANY)
-    scalars = pl.BlockSpec(memory_space=pltpu.SMEM)
+    held = pl.BlockSpec(memory_space=pltpu.HBM)
     rounds = ITERS + 1
     dma = pltpu.SemaphoreType.DMA
     deep = fields * rows
@@ -377,9 +388,13 @@
             jax.ShapeDtypeStruct(dist.shape, bf16),
             jax.ShapeDtypeStruct((rounds, fields), f32),
         ),
-        in_specs=[anywhere] * 4 + [scalars] * 4,
+        in_specs=[held] * 8,
         out_specs=(anywhere, pl.BlockSpec(memory_space=pltpu.VMEM)),
         scratch_shapes=[
+            pltpu.SMEM((fields, fields), f32),
+            pltpu.SMEM((fields, fields), f32),
+            pltpu.SMEM((fields,), f32),
+            pltpu.SMEM((fields,), f32),
             pltpu.VMEM((nv, vel, rows, lanes), f32),
             pltpu.VMEM((nv, vel, rows, lanes), bf16),
             pltpu.VMEM((CHUNKS, vel // CHUNKS, rows, lanes), f32),
@@ -399,7 +414,7 @@
             pltpu.VMEM((lanes, lanes), f32),
             pltpu.VMEM((ncx * nv, rows, lanes), f32),
             pltpu.VMEM((ncyz, rows, lanes), f32),
-            dma((nv,)), dma((3,)), dma((nv,)), dma((nv,)),
+            dma((nv,)), dma((7,)), dma((nv,)), dma((nv,)),
             dma((rounds, 4)), dma((rounds, 4)), dma((nv,)), dma((nv,)),
             dma((ncx * nv,)), dma((ncx * nv,)), dma((ncyz,)), dma((ncyz,)), dma((nv,)),
         ],

time: 39.5 us -> 38.6 us (0.977)
  Pallas kernels: 33.7 us -> 32.8 us
    pallas_call x1, Pallas kernels: 33.7 us -> 32.8 us  [local(): pl.pallas_call(functools.partial(kernel, sizes), out_shape=(jax.ShapeDtyp...]
where the time goes in v3:
time: 38.6 us; the launch traced here: 38.4 us
  Pallas kernels  32.8 us (85%)
  local copies, waits for them, and re-layouts  5 us (13%)
  between operations  0.65 us (2%)
    pallas_call x1, Pallas kernels, local(): pl.pallas_call(functools.partial(kernel, sizes), out_shape=(jax.ShapeDtyp...  32.8 us
    unnamed x4, local copies, waits for them, and re-layouts  5 us

profile of v3, /device:TPU:0, one launch (start us, length us, event | category | flops | bytes accessed | tf_op | source)
XLA Modules:
  0.0 38.4 jit_solution(5352743496698785650)
XLA Ops:
  0.6 32.8 %shard_map.95 = (bf16[432,4,8,128]{3,2,1,0:T(8,128)(2,1)}, f32[5,13]{1,0:T(8,128)}) custom-call(f32[432,4,8,128]{3,2,1,0:T(8,128)} %dist.1, s32[4,8,128]{2,1,0:T(8,128)} %cell_type.1, f32[13,432]{1,0:T(8,128)} %basis.1, f32[13,432]{1,0:T(8,128)} %bitcast.1, f32[13,13]{1,0:T(8,128)} %source_hbm.1, f32[13,13]{1,0:T(8,128)} %coupling_hbm.1, f32[13]{0:T(128)} %diffusivity_hbm.1, ...), custom_call_target="tpu_custom_call" | custom-call | tf_op jit(solution)/shard_map/pallas_call | solution.py:385
  33.4 0.0 copy-start
  33.4 4.4 %copy.12 = bf16[432,4,8,128]{3,2,1,0:T(8,128)(2,1)} copy(bf16[432,4,8,128]{3,2,1,0:T(8,128)(2,1)} %get-tuple-element.4) | data formatting | bytes 7077888
  37.8 0.0 copy-done
  37.8 0.6 %copy.13 = f32[5,13]{1,0:T(8,128)} copy(f32[5,13]{1,0:T(8,128)S(1)} %copy-done) | data formatting | bytes 520
Async XLA Ops:
  33.4 4.4 %copy-start = (f32[5,13]{1,0:T(8,128)S(1)}, f32[5,13]{1,0:T(8,128)}, u32[]{:S(2)}) copy-start(f32[5,13]{1,0:T(8,128)} %get-tuple-element.5) | copy-start | bytes 784

commit v4 on v3

--- a/solution.py
+++ b/solution.py
@@ -24,9 +24,9 @@
 def kernel(
     sizes, dist, cell_type, basis, backmap, source_hbm, coupling_hbm, diffusivity_hbm, gain_hbm,
     out, norms,
-    source_map, coupling, diffusivity, gain, dist_v, out_v, delta_v, cells_v, basis_v, wide_v, back_v, backw_v, backs_v,
+    source_map, coupling, diffusivity, gain, dist_v, delta_v, cells_v, basis_v, wide_v, back_v, backw_v, backs_v,
     part, arrived, field, xh, ystage, yh, planes_v, sq, first, second,
-    dist_sem, small_sem, rs_s, rs_r, h_s, h_r, ag_s, ag_r, a1_s, a1_r, a2_s, a2_r, out_sem,
+    dist_sem, small_sem, rs_s, rs_r, h_s, h_r, ag_s, ag_r, a1_s, a1_r, a2_s, a2_r,
 ):
     ncx, ncyz, nv, fields, vel, rows, lanes = sizes
     cx, cyz, me = lax.axis_index("cx"), lax.axis_index("cyz"), lax.axis_index("vert")
@@ -284,7 +284,6 @@
     coupled = mix(coupling, correction)
 
     size = vel // CHUNKS
-    stores = []
 
     def finish(step):
         owner = order[step]
@@ -307,10 +306,7 @@
                 )
                 for i in range(2):
                     flat[pl.ds(y + i, size, stride=rows), :] = delta[:, i * lanes:(i + 1) * lanes]
-            out_v[step, span] = (dist_v[step, span] + delta_v[chunk]).astype(bf16)
-        copy = pltpu.make_async_copy(out_v.at[step], out.at[:, plane_of(owner)], out_sem.at[step])
-        copy.start()
-        stores.append(copy)
+            out[span, plane_of(owner)] = (dist_v[step, span] + delta_v[chunk]).astype(bf16)
 
     finish(last)
     wait_halo(ITERS)
@@ -366,8 +362,6 @@
         sum_first(mine, index, (cx + dx) % ncx, (me + dv) % nv).wait_send()
     for dy in range(1, ncyz):
         sum_second(cyz, dy, (cyz + dy) % ncyz).wait_send()
-    for copy in stores:
-        copy.wait()
 
 
 def local(mesh_shape, *args):
@@ -377,7 +371,6 @@
     fields = basis.shape[0]
     assert planes == nv and nv % 2 == 0 and vel % (CHUNKS * 16) == 0
     sizes = (ncx, ncyz, nv, fields, vel, rows, lanes)
-    anywhere = pl.BlockSpec(memory_space=pl.ANY)
     held = pl.BlockSpec(memory_space=pltpu.HBM)
     rounds = ITERS + 1
     dma = pltpu.SemaphoreType.DMA
@@ -385,18 +378,17 @@
     return pl.pallas_call(
         functools.partial(kernel, sizes),
         out_shape=(
-            jax.ShapeDtypeStruct(dist.shape, bf16),
+            pltpu.VMEM(dist.shape, bf16),
             jax.ShapeDtypeStruct((rounds, fields), f32),
         ),
         in_specs=[held] * 8,
-        out_specs=(anywhere, pl.BlockSpec(memory_space=pltpu.VMEM)),
+        out_specs=(pl.BlockSpec(memory_space=pltpu.VMEM),) * 2,
         scratch_shapes=[
             pltpu.SMEM((fields, fields), f32),
             pltpu.SMEM((fields, fields), f32),
             pltpu.SMEM((fields,), f32),
             pltpu.SMEM((fields,), f32),
             pltpu.VMEM((nv, vel, rows, lanes), f32),
-            pltpu.VMEM((nv, vel, rows, lanes), bf16),
             pltpu.VMEM((CHUNKS, vel // CHUNKS, rows, lanes), f32),
             pltpu.VMEM(cell_type.shape, jnp.int32),
             pltpu.VMEM((fields, vel), f32),
@@ -416,10 +408,10 @@
             pltpu.VMEM((ncyz, rows, lanes), f32),
             dma((nv,)), dma((7,)), dma((nv,)), dma((nv,)),
             dma((rounds, 4)), dma((rounds, 4)), dma((nv,)), dma((nv,)),
-            dma((ncx * nv,)), dma((ncx * nv,)), dma((ncyz,)), dma((ncyz,)), dma((nv,)),
+            dma((ncx * nv,)), dma((ncx * nv,)), dma((ncyz,)), dma((ncyz,)),
         ],
         compiler_params=pltpu.CompilerParams(
-            collective_id=0, has_side_effects=True, vmem_limit_bytes=67043328
+            collective_id=0, has_side_effects=True, vmem_limit_bytes=58 * 10**6
         ),
     )(*args[:3], args[3].T, *args[4:])
 

time: 38.6 us -> 35.9 us (0.930)
  local copies, waits for them, and re-layouts: 5 us -> 2.39 us
    unnamed x4, local copies, waits for them, and re-layouts: 5 us -> 2.39 us
where the time goes in v4:
time: 35.9 us; the launch traced here: 35.8 us
  Pallas kernels  32.7 us (91%)
  local copies, waits for them, and re-layouts  2.39 us (7%)
  between operations  0.65 us (2%)
    pallas_call x1, Pallas kernels, local(): pl.pallas_call(functools.partial(kernel, sizes), out_shape=(pltpu.VMEM(di...  32.7 us
    unnamed x4, local copies, waits for them, and re-layouts  2.39 us

profile of v4, /device:TPU:0, one launch (start us, length us, event | category | flops | bytes accessed | tf_op | source)
XLA Modules:
  0.0 35.8 jit_solution(382747736630063033)
XLA Ops:
  0.6 32.7 %shard_map.95 = (bf16[432,4,8,128]{3,2,1,0:T(8,128)(2,1)S(1)}, f32[5,13]{1,0:T(8,128)}) custom-call(f32[432,4,8,128]{3,2,1,0:T(8,128)} %dist.1, s32[4,8,128]{2,1,0:T(8,128)} %cell_type.1, f32[13,432]{1,0:T(8,128)} %basis.1, f32[13,432]{1,0:T(8,128)} %bitcast.1, f32[13,13]{1,0:T(8,128)} %source_hbm.1, f32[13,13]{1,0:T(8,128)} %coupling_hbm.1, ...), custom_call_target="tpu_custom_call" | custom-call | tf_op jit(solution)/shard_map/pallas_call | solution.py:378
  33.4 0.0 copy-start
  33.4 1.8 %copy.12 = bf16[432,4,8,128]{3,2,1,0:T(8,128)(2,1)} copy(bf16[432,4,8,128]{3,2,1,0:T(8,128)(2,1)S(1)} %get-tuple-element.2) | data formatting | bytes 7077888
  35.2 0.0 copy-done
  35.2 0.6 %copy.13 = f32[5,13]{1,0:T(8,128)} copy(f32[5,13]{1,0:T(8,128)S(1)} %copy-done) | data formatting | bytes 520
Async XLA Ops:
  33.4 1.8 %copy-start = (f32[5,13]{1,0:T(8,128)S(1)}, f32[5,13]{1,0:T(8,128)}, u32[]{:S(2)}) copy-start(f32[5,13]{1,0:T(8,128)} %get-tuple-element.7) | copy-start | bytes 784
